TPU v7x, 32 devices: a whole 2x2x4 slice. The times are simulated.
32 devices in a mesh: dp: 8 (over y, x, core), tensor: 4 (over z).
Axes of the slice: x: 2, y: 2, z: 4, core: 2. Of those that a mesh axis runs over, the one named last changes fastest.
Arguments:
- tokens: bfloat16 [16384, 768], P(('dp', 'tensor')), may hold values from -6 to 6
- starts: int32 [8, 8], P('dp'), may hold values from 0 to 2047, as said below
- w_qkv: bfloat16 [768, 2304], P(None, 'tensor'), may hold values from -0.21875 to 0.21875
- b_qkv: bfloat16 [2304], P('tensor'), may hold values from -3 to 3
- w_out: bfloat16 [768, 768], P('tensor'), may hold values from -2 to 2
- b_out: bfloat16 [768], replicated, may hold values from -3 to 3
- gain_one: bfloat16 [768], replicated, may hold values from 0.099609375 to 1.8984375
- shift_one: bfloat16 [768], replicated, may hold values from -3 to 3
- w_in: bfloat16 [768, 3072], P(None, 'tensor'), may hold values from -0.21875 to 0.21875
- b_in: bfloat16 [3072], P('tensor'), may hold values from -3 to 3
- w_two: bfloat16 [3072, 768], P('tensor'), may hold values from -0.21875 to 0.21875
- b_two: bfloat16 [768], replicated, may hold values from -3 to 3
- gain_two: bfloat16 [768], replicated, may hold values from 0.099609375 to 1.8984375
- shift_two: bfloat16 [768], replicated, may hold values from -3 to 3
- cotangent: bfloat16 [16384, 768], P(('dp', 'tensor')), may hold values from -6 to 6
Outputs:
- block_out: bfloat16 [16384, 768], P(('dp', 'tensor'))
- d_tokens: bfloat16 [16384, 768], P(('dp', 'tensor'))
- d_w_qkv: float32 [768, 2304], P(None, 'tensor')
- d_b_qkv: float32 [2304], P('tensor')
- d_w_out: float32 [768, 768], P('tensor')
- d_b_out: float32 [768], replicated
- d_gain_one: float32 [768], replicated
- d_shift_one: float32 [768], replicated
- d_w_in: float32 [768, 3072], P(None, 'tensor')
- d_b_in: float32 [3072], P('tensor')
- d_w_two: float32 [3072, 768], P('tensor')
- d_b_two: float32 [768], replicated
- d_gain_two: float32 [768], replicated
- d_shift_two: float32 [768], replicated
Inputs may be any that keep to these rules, and one draw needn't show every extreme that they name: Each row holds exactly 8 documents: its first start is 0 and its starts rise strictly. In the first row the last document is a single token.
All inputs are finite; a program needn't handle non-finite values.
Results may differ from a plain program's by a relative error of at most 0.014.
Values may be sent and summed in bfloat16 or wider, within the bound.
No kernel may reach another device: no remote copies, remote signals or barrier semaphores. Data moves between devices by JAX's collectives and lax.ppermute only.
A program may use at most 192 MiB of HBM per device.

v0:
```python
import math
import jax
import jax.numpy as jnp
from jax import lax
from jax.sharding import PartitionSpec as P

HEAD = 64
GROUP = 64
ROW_LEN = 2048
DOCS = 8
highest = lax.Precision.HIGHEST


def doc_tables(starts_row):
    places = jnp.arange(ROW_LEN, dtype=jnp.int32)
    started = (places[:, None] >= starts_row[None, :]).astype(jnp.int32)
    doc_ids = jnp.sum(started, axis=1) - 1
    onehot = (doc_ids[:, None] == jnp.arange(DOCS, dtype=jnp.int32)[None, :]).astype(jnp.int32)
    finish = jnp.concatenate([starts_row[1:], jnp.full((1,), ROW_LEN, jnp.int32)])
    own_start = jnp.sum(onehot * starts_row[None, :], axis=1)
    own_len = jnp.sum(onehot * (finish - starts_row)[None, :], axis=1)
    angles = 0.5 * math.pi * (places - own_start).astype(jnp.float32) / own_len.astype(jnp.float32)
    return (angles, doc_ids)


def attend(mixed, angles, doc_ids):
    length = mixed.shape[0]
    head_count = mixed.shape[1] // (3 * HEAD)
    blocks = length // GROUP
    pieces = mixed.reshape(blocks, GROUP, head_count, 3, HEAD)
    queries = jax.nn.relu(pieces[:, :, :, 0])
    key_pos = jax.nn.relu(pieces[:, :, :, 1])
    values = pieces[:, :, :, 2]
    cosine = jnp.cos(angles).reshape(blocks, GROUP, 1, 1)
    sines = jnp.sin(angles).reshape(blocks, GROUP, 1, 1)
    query_feat = jnp.concatenate([queries * cosine, queries * sines], axis=-1)
    key_feat = jnp.concatenate([key_pos * cosine, key_pos * sines], axis=-1)
    doc_blocks = doc_ids.reshape(blocks, GROUP)
    within = jnp.arange(GROUP, dtype=jnp.int32)
    inside_mask = (
        (doc_blocks[:, :, None] == doc_blocks[:, None, :])
        & (within[None, :, None] >= within[None, None, :])
    ).astype(jnp.float32)
    scores = (
        jnp.einsum("bihf,bjhf->bhij", query_feat, key_feat, precision=highest)
        * inside_mask[:, None]
    )
    numerator = jnp.einsum("bhij,bjhd->bihd", scores, values, precision=highest)
    denominator = jnp.transpose(jnp.sum(scores, axis=-1), (0, 2, 1))
    first_doc = doc_blocks[:, 0]
    last_doc = doc_blocks[:, -1]
    tail_mask = (doc_blocks == last_doc[:, None]).astype(jnp.float32)
    states = jnp.einsum("bjhf,bjhd,bj->bhfd", key_feat, values, tail_mask, precision=highest)
    key_sums = jnp.einsum("bjhf,bj->bhf", key_feat, tail_mask, precision=highest)
    order = jnp.arange(blocks, dtype=jnp.int32)
    link_mask = (
        (last_doc[None, :] == first_doc[:, None]) & (order[None, :] < order[:, None])
    ).astype(jnp.float32)
    carried = jnp.einsum("cb,bhfd->chfd", link_mask, states, precision=highest)
    carried_sum = jnp.einsum("cb,bhf->chf", link_mask, key_sums, precision=highest)
    opening = (doc_blocks == first_doc[:, None]).astype(jnp.float32)
    numerator = numerator + jnp.einsum(
        "bihf,bhfd,bi->bihd", query_feat, carried, opening, precision=highest
    )
    denominator = denominator + jnp.einsum(
        "bihf,bhf,bi->bih", query_feat, carried_sum, opening, precision=highest
    )
    result = numerator / jnp.maximum(denominator, 1.0)[..., None]
    return result.reshape(length, head_count * HEAD)


def attend_rows(mixed, angles, doc_ids):
    row_count = angles.shape[0]
    shaped = mixed.reshape(row_count, angles.shape[1], mixed.shape[1])
    return jax.vmap(attend)(shaped, angles, doc_ids).reshape(mixed.shape[0], -1)


def normalize(rows_in, gain, shift):
    centred = rows_in - jnp.mean(rows_in, axis=-1, keepdims=True)
    spread = jnp.mean(centred * centred, axis=-1, keepdims=True)
    return centred * lax.rsqrt(spread + 1e-05) * gain + shift


def smooth(values):
    return jax.nn.gelu(values)


def inner_rows(left, right):
    return lax.dot_general(
        left, right, (((0,), (0,)), ((), ())), preferred_element_type=jnp.float32
    )


def times_rows(left, right):
    return lax.dot_general(
        left, right, (((1,), (1,)), ((), ())), preferred_element_type=jnp.float32
    )


def rows_product(source, weight):
    return jnp.dot(source, weight, preferred_element_type=jnp.float32)


def rows_back(source, weight):
    return times_rows(source, weight)


def on_device(
    tokens,
    starts,
    w_qkv,
    b_qkv,
    w_out,
    b_out,
    gain_one,
    shift_one,
    w_in,
    b_in,
    w_two,
    b_two,
    gain_two,
    shift_two,
    cotangent,
):
    angles, doc_ids = jax.vmap(doc_tables)(starts)
    bias_qkv = b_qkv.astype(jnp.float32)
    bias_in = b_in.astype(jnp.float32)
    gain_a = gain_one.astype(jnp.float32)
    shift_a = shift_one.astype(jnp.float32)
    gain_b = gain_two.astype(jnp.float32)
    shift_b = shift_two.astype(jnp.float32)
    input_full = lax.all_gather(tokens, "tensor", axis=0, tiled=True)
    mixed = jnp.dot(input_full, w_qkv, preferred_element_type=jnp.float32) + bias_qkv
    attended = attend_rows(mixed, angles, doc_ids).astype(jnp.bfloat16)
    branch = lax.psum_scatter(
        rows_product(attended, w_out), "tensor", scatter_dimension=0, tiled=True
    ) + b_out.astype(jnp.float32)
    first_sum = tokens.astype(jnp.float32) + branch
    first_low = normalize(first_sum, gain_a, shift_a).astype(jnp.bfloat16)
    middle_full = lax.all_gather(first_low, "tensor", axis=0, tiled=True)
    hidden = jnp.dot(middle_full, w_in, preferred_element_type=jnp.float32) + bias_in
    active = smooth(hidden).astype(jnp.bfloat16)
    second = lax.psum_scatter(
        rows_product(active, w_two), "tensor", scatter_dimension=0, tiled=True
    ) + b_two.astype(jnp.float32)
    second_sum = first_low.astype(jnp.float32) + second
    block_out = normalize(second_sum, gain_b, shift_b).astype(jnp.bfloat16)
    input_back = lax.all_gather(tokens, "tensor", axis=0, tiled=True)
    middle_back = lax.all_gather(first_low, "tensor", axis=0, tiled=True)
    unused_two, norm_two_back = jax.vjp(normalize, second_sum, gain_b, shift_b)
    d_r2, d_gain_two, d_shift_two = norm_two_back(cotangent.astype(jnp.float32))
    d_second = d_r2.astype(jnp.bfloat16)
    d_b_two = jnp.sum(d_second, axis=0, dtype=jnp.float32)
    second_full = lax.all_gather(d_second, "tensor", axis=0, tiled=True)
    hidden_again = jnp.dot(middle_back, w_in, preferred_element_type=jnp.float32) + bias_in
    active_val, gelu_back = jax.vjp(smooth, hidden_again)
    active_again = active_val.astype(jnp.bfloat16)
    d_w_two = inner_rows(active_again, second_full)
    d_active = times_rows(second_full, w_two)
    d_hidden = gelu_back(d_active)[0].astype(jnp.bfloat16)
    d_b_in = jnp.sum(d_hidden, axis=0, dtype=jnp.float32)
    d_w_in = inner_rows(middle_back, d_hidden)
    d_first = (
        lax.psum_scatter(rows_back(d_hidden, w_in), "tensor", scatter_dimension=0, tiled=True)
        + d_r2
    )
    unused_one, norm_one_back = jax.vjp(normalize, first_sum, gain_a, shift_a)
    d_r1, d_gain_one, d_shift_one = norm_one_back(d_first)
    d_branch = d_r1.astype(jnp.bfloat16)
    d_b_out = jnp.sum(d_branch, axis=0, dtype=jnp.float32)
    branch_full = lax.all_gather(d_branch, "tensor", axis=0, tiled=True)
    mixed_again = jnp.dot(input_back, w_qkv, preferred_element_type=jnp.float32) + bias_qkv
    attended_val, attend_back = jax.vjp(
        lambda mixed_in: attend_rows(mixed_in, angles, doc_ids), mixed_again
    )
    attended_again = attended_val.astype(jnp.bfloat16)
    d_w_out = inner_rows(attended_again, branch_full)
    d_attended = times_rows(branch_full, w_out)
    d_mixed = attend_back(d_attended)[0].astype(jnp.bfloat16)
    d_b_qkv = jnp.sum(d_mixed, axis=0, dtype=jnp.float32)
    d_w_qkv = inner_rows(input_back, d_mixed)
    d_tokens = (
        lax.psum_scatter(
            rows_back(d_mixed, w_qkv).astype(jnp.bfloat16),
            "tensor",
            scatter_dimension=0,
            tiled=True,
        ).astype(jnp.float32)
        + d_r1
    ).astype(jnp.bfloat16)
    d_w_qkv, d_b_qkv, d_w_out, d_w_in, d_b_in, d_w_two = lax.psum(
        (d_w_qkv, d_b_qkv, d_w_out, d_w_in, d_b_in, d_w_two), "dp"
    )
    d_b_out, d_gain_one, d_shift_one, d_b_two, d_gain_two, d_shift_two = lax.psum(
        (d_b_out, d_gain_one, d_shift_one, d_b_two, d_gain_two, d_shift_two), ("dp", "tensor")
    )
    return (
        block_out,
        d_tokens,
        d_w_qkv,
        d_b_qkv,
        d_w_out,
        d_b_out,
        d_gain_one,
        d_shift_one,
        d_w_in,
        d_b_in,
        d_w_two,
        d_b_two,
        d_gain_two,
        d_shift_two,
    )


def solution(mesh):
    in_specs = (
        P(("dp", "tensor"), None),
        P("dp", None),
        P(None, "tensor"),
        P("tensor"),
        P("tensor", None),
        P(),
        P(),
        P(),
        P(None, "tensor"),
        P("tensor"),
        P("tensor", None),
        P(),
        P(),
        P(),
        P(("dp", "tensor"), None),
    )
    out_specs = (
        P(("dp", "tensor"), None),
        P(("dp", "tensor"), None),
        P(None, "tensor"),
        P("tensor"),
        P("tensor", None),
        P(),
        P(),
        P(),
        P(None, "tensor"),
        P("tensor"),
        P("tensor", None),
        P(),
        P(),
        P(),
    )
    return jax.shard_map(
        on_device, mesh=mesh, in_specs=in_specs, out_specs=out_specs, check_vma=False
    )
```

profile of v0, /device:TPU:0, one launch (start us, length us, event | category | flops | bytes accessed | tf_op | source)
XLA Modules:
  0.0 1038.7 jit_solution(10530214980209661449)
XLA Ops:
  12.7 63.1 %all-gather.5.cloned.1.call-done = bf16[2048,768]{1,0:T(8,128)(2,1)} async-done(((bf16[512,768]{1,0:T(8,128)(2,1)}), bf16[2048,768]{1,0:T(8,128)(2,1)}) %all-gather.5.cloned.1.call-update) | async-done | bytes 3145744 | tf_op jit(solution)/shard_map/all_gather | solution.py:132
  75.8 6.3 convolution_add_fusion
  82.2 8.7 reshape_reshape.3
  90.9 8.2 fusion.101
  99.1 3.9 copy.193
  103.0 3.9 copy.191
  106.9 3.9 copy.192
  110.8 5.1 bitcast_multiply_fusion.4
  115.8 3.8 maximum_bitcast_fusion
  121.2 2.6 copy-done.6
  123.8 6.0 fusion.31
  129.9 4.1 fusion.28
  134.0 5.0 fusion.78
  139.0 5.4 multiply_reduce_fusion.1
  144.4 5.4 fusion.24
  150.5 9.1 divide_convert_fusion
  160.7 1.7 convert_element_type.153
  162.4 4.9 fusion.102
  169.7 107.1 %reduce-scatter.5.cloned.1.call-done = f32[512,768]{1,0:T(8,128)} async-done(((f32[2048,768]{1,0:T(8,128)}), f32[512,768]{1,0:T(8,128)}) %reduce-scatter.5.cloned.1.call-update) | async-done | bytes 1572880 | tf_op jit(solution)/shard_map/reduce_scatter | solution.py:135
  276.8 1.7 fusion.99
  280.2 64.1 %all-gather.7.cloned.1.call-done = bf16[2048,768]{1,0:T(8,128)(2,1)} async-done(((bf16[512,768]{1,0:T(8,128)(2,1)}), bf16[2048,768]{1,0:T(8,128)(2,1)}) %all-gather.7.cloned.1.call-update) | async-done | bytes 3145744 | tf_op jit(solution)/shard_map/all_gather | solution.py:140
  344.3 8.4 multiply_convert_fusion
  352.7 1.7 copy-done.88
  354.4 4.4 fusion.103
  361.3 107.1 %reduce-scatter.7.cloned.1.call-done = f32[512,768]{1,0:T(8,128)} async-done(((f32[2048,768]{1,0:T(8,128)}), f32[512,768]{1,0:T(8,128)}) %reduce-scatter.7.cloned.1.call-update) | async-done | bytes 1572880 | tf_op jit(solution)/shard_map/reduce_scatter | solution.py:143
  468.4 2.0 fusion.98
  474.7 1.7 convert_reduce_fusion.3
  476.5 64.1 %all-gather.9.cloned.1.call-done = bf16[2048,768]{1,0:T(8,128)(2,1)} async-done(((bf16[512,768]{1,0:T(8,128)(2,1)}), bf16[2048,768]{1,0:T(8,128)(2,1)}) %all-gather.9.cloned.1.call-update) | async-done | bytes 3145744 | tf_op jit(solution)/shard_map/all_gather | solution.py:154
  540.6 9.8 convert_reduce_fusion.1
  550.4 1.6 copy-done.89
  552.1 4.5 fusion.104
  556.7 109.5 %reduce-scatter.9.cloned.1.call-done = f32[512,768]{1,0:T(8,128)} async-done(((f32[2048,768]{1,0:T(8,128)}), f32[512,768]{1,0:T(8,128)}) %reduce-scatter.9.cloned.1.call-update) | async-done | bytes 1572880 | tf_op jit(solution)/shard_map/reduce_scatter | solution.py:164
  666.2 3.3 multiply_reduce_fusion.2
  671.3 1.7 convert_reduce_fusion.4
  673.7 63.5 %all-gather.11.cloned.1.call-done = bf16[2048,768]{1,0:T(8,128)(2,1)} async-done(((bf16[512,768]{1,0:T(8,128)(2,1)}), bf16[2048,768]{1,0:T(8,128)(2,1)}) %all-gather.11.cloned.1.call-update) | async-done | bytes 3145744 | tf_op jit(solution)/shard_map/all_gather | solution.py:171
  737.2 3.1 fusion.105
  740.3 2.6 reshape.798
  742.9 12.0 %fusion.21 = f32[32,3,64,64]{2,3,1,0:T(8,128)} fusion(f32[32,3,64,64]{2,3,1,0:T(8,128)} %copy-done.21, f32[32,64,64]{1,2,0:T(8,128)S(1)} %copy-done.12, f32[1,32,64,3,64]{2,1,4,3,0:T(8,128)} %reshape.798, f32[32,64,3]{1,2,0:T(4,128)S(1)} %copy-done.42), kind=kOutput, calls=%fused_computation.38 | convolution fusion | flops 302776320 | bytes 5267456 | tf_op jit(solution)/shard_map/transpose(jvp(vmap(bhij,bjhd->bihd)))/dot_general | solution.py:48
  754.9 7.4 fusion.19
  762.3 2.4 reshape.793
  764.7 5.4 multiply_reduce_fusion
  770.2 2.7 fusion.76
  773.2 4.0 copy.158
  777.2 8.3 fusion.42
  785.6 3.7 fusion.45
  789.3 5.8 fusion.30
  795.2 7.7 fusion.13
  802.9 7.0 fusion.38
  810.0 4.6 bitcast_add_fusion
  814.7 8.1 add_bitcast_fusion
  822.8 2.8 fusion.12
  825.6 2.8 convert_reduce_fusion
  828.5 7.4 copy.171
  835.9 6.7 convert_element_type.170
  842.5 4.1 convolution_convert_fusion
  847.0 7.1 fusion.108
  854.1 4.2 fusion.107
  858.3 1.6 fusion.106
  860.4 3.2 convolution_bitcast_fusion
  864.5 43.0 %all-reduce.3 = (f32[768]{0:T(1024)}, f32[768]{0:T(1024)}, f32[768]{0:T(1024)}, f32[768]{0:T(1024)}, f32[768]{0:T(1024)}, /*index=5*/f32[768]{0:T(1024)}) all-reduce(f32[768]{0:T(1024)S(1)} %copy-done.71, f32[768]{0:T(1024)S(1)} %copy-done.72, f32[768]{0:T(1024)S(1)} %copy-done.73, ...), channel_id=1, replica_groups=mesh['dp'=8,'tensor'=4] {'dp','tensor'}, use_global_device_ids=true, to_apply=%region_22.23 | all-reduce | flops 4608 | bytes 36864 | tf_op jit(solution)/shard_map/psum | solution.py:194
  907.5 14.0 %all-reduce.4 = (f32[576]{0:T(1024)}, f32[768]{0:T(1024)}) all-reduce(f32[576]{0:T(1024)S(1)} %reduce_sum.223, f32[768]{0:T(1024)S(1)} %copy-done.76), channel_id=1, replica_groups=mesh['dp'=8,'tensor'=4] {'dp'}, use_global_device_ids=true, to_apply=%region_19.20 | all-reduce | flops 1344 | bytes 10752 | tf_op jit(solution)/shard_map/psum | solution.py:191
  921.5 2.3 add_convert_fusion.1
  923.8 101.3 %all-reduce.8.cloned.1.call-done = (f32[768,576]{0,1:T(8,128)}, f32[192,768]{1,0:T(8,128)}, f32[768,768]{1,0:T(8,128)}, f32[768,768]{1,0:T(8,128)}) async-done(((f32[768,576]{0,1:T(8,128)}, f32[192,768]{1,0:T(8,128)}, f32[768,768]{1,0:T(8,128)}, f32[768,768]{1,0:T(8,128)}), (f32[768,576]{0,1:T(8,128)}, f32[192,768]{1,0:T(8,128)}, f32[768,768]{1,0:T(8,128)}, ...) | async-done | bytes 7077904 | tf_op jit(solution)/shard_map/psum | solution.py:191
  1025.1 2.9 copy.250
  (249 shorter events, 27.9 us)
Async XLA Ops:
  7.2 337.2 %copy-start = (bf16[768,768]{1,0:T(8,128)(2,1)S(1)}, bf16[768,768]{1,0:T(8,128)(2,1)}, u32[]{:S(2)}) copy-start(bf16[768,768]{1,0:T(8,128)(2,1)} %param.23) | copy-start | bytes 3538948
  7.2 68.6 %all-gather.5.cloned.1.call-start = ((), (), s32[]{:S(2)}) async-start(), calls=%async_computation.4 | async-start | bytes 3932160 | tf_op jit(solution)/shard_map/all_gather | solution.py:132
  7.9 268.9 %reduce-scatter.5.cloned.1.call-start = ((), (), s32[]{:S(2)}) async-start(), calls=%async_computation.5 | async-start | bytes 7864320 | tf_op jit(solution)/shard_map/reduce_scatter | solution.py:135
  12.1 117.7 %copy-start.61 = (s32[32]{0:T(128)}, s32[32]{0:T(128)S(1)}, u32[]{:S(2)}) copy-start(s32[32]{0:T(128)S(1)} %get-tuple-element.20) | copy-start | bytes 388
  12.1 117.7 %copy-start.64 = (s32[32]{0:T(128)}, s32[32]{0:T(128)S(1)}, u32[]{:S(2)}) copy-start(s32[32]{0:T(128)S(1)} %get-tuple-element.21) | copy-start | bytes 388
  12.2 109.0 %copy-start.39 = (f32[32,64]{1,0:T(8,128)}, f32[32,64]{1,0:T(8,128)S(1)}, u32[]{:S(2)}) copy-start(f32[32,64]{1,0:T(8,128)S(1)} %get-tuple-element.57) | copy-start | bytes 24580
  12.3 98.5 %copy-start.44 = (f32[32,64]{1,0:T(8,128)}, f32[32,64]{1,0:T(8,128)S(1)}, u32[]{:S(2)}) copy-start(f32[32,64]{1,0:T(8,128)S(1)} %get-tuple-element.71) | copy-start | bytes 24580
  12.3 98.4 %copy-start.46 = (f32[32,64]{1,0:T(8,128)}, f32[32,64]{1,0:T(8,128)S(1)}, u32[]{:S(2)}) copy-start(f32[32,64]{1,0:T(8,128)S(1)} %get-tuple-element.72) | copy-start | bytes 24580
  12.7 131.7 %copy-start.11 = (f32[32,64,64]{1,2,0:T(8,128)}, f32[32,64,64]{1,2,0:T(8,128)S(1)}, u32[]{:S(2)}) copy-start(f32[32,64,64]{1,2,0:T(8,128)S(1)} %and_convert_fusion) | copy-start | bytes 1572868
  119.6 19.4 %copy-start.4 = (f32[32,64,3,128]{3,1,2,0:T(8,128)}, f32[32,64,3,128]{3,1,2,0:T(8,128)S(1)}, u32[]{:S(2)}) copy-start(f32[32,64,3,128]{3,1,2,0:T(8,128)S(1)} %get-tuple-element.81) | copy-start | bytes 9437188
  119.6 30.9 %copy-start.2 = (f32[32,64,3,128]{3,1,2,0:T(8,128)}, f32[32,64,3,128]{3,1,2,0:T(8,128)S(1)}, u32[]{:S(2)}) copy-start(f32[32,64,3,128]{3,1,2,0:T(8,128)S(1)} %get-tuple-element.80) | copy-start | bytes 9437188
  121.2 12.8 %copy-start.35 = (f32[32,3,128]{2,0,1:T(8,128)}, f32[32,3,128]{2,0,1:T(8,128)S(1)}, u32[]{:S(2)}) copy-start(f32[32,3,128]{2,0,1:T(8,128)S(1)} %fusion.73) | copy-start | bytes 147460
  134.0 16.5 %copy-start.19 = (f32[32,3,128,64]{2,0,3,1:T(8,128)}, f32[32,3,128,64]{2,0,3,1:T(8,128)S(1)}, u32[]{:S(2)}) copy-start(f32[32,3,128,64]{2,0,3,1:T(8,128)S(1)} %fusion.28) | copy-start | bytes 9437188
  139.0 10.9 %copy-start.37 = (f32[32,3,1,64]{3,2,1,0:T(1,128)}, f32[32,3,1,64]{3,2,1,0:T(1,128)S(1)}, u32[]{:S(2)}) copy-start(f32[32,3,1,64]{3,2,1,0:T(1,128)S(1)} %fusion.78) | copy-start | bytes 73732
  144.4 5.5 copy-start.21
  144.4 5.5 copy-start.32
  150.5 9.1 copy-start.41
  162.4 4.9 copy-start.23
  167.2 109.6 %copy-start.27 = (bf16[512,768]{1,0:T(8,128)(2,1)S(1)}, bf16[512,768]{1,0:T(8,128)(2,1)}, u32[]{:S(2)}) copy-start(bf16[512,768]{1,0:T(8,128)(2,1)} %param.15) | copy-start | bytes 2359300
  167.3 177.1 %all-gather.7.cloned.1.call-start = ((), (), s32[]{:S(2)}) async-start(), calls=%async_computation.6 | async-start | bytes 3932160 | tf_op jit(solution)/shard_map/all_gather | solution.py:140
  278.6 74.1 %copy-start.50 = (f32[512]{0:T(512)}, f32[512]{0:T(512)S(1)}, u32[]{:S(2)}) copy-start(f32[512]{0:T(512)S(1)} %broadcast_multiply_fusion.1) | copy-start | bytes 6148
  278.9 73.8 %copy-start.57 = (f32[512]{0:T(512)}, f32[512]{0:T(512)S(1)}, u32[]{:S(2)}) copy-start(f32[512]{0:T(512)S(1)} %multiply_reduce_fusion.5) | copy-start | bytes 6148
  278.9 73.8 %copy-start.53 = (f32[512]{0:T(512)}, f32[512]{0:T(512)S(1)}, u32[]{:S(2)}) copy-start(f32[512]{0:T(512)S(1)} %fusion.86) | copy-start | bytes 6148
  280.2 188.3 %reduce-scatter.7.cloned.1.call-start = ((), (), s32[]{:S(2)}) async-start(), calls=%async_computation.7 | async-start | bytes 7864320 | tf_op jit(solution)/shard_map/reduce_scatter | solution.py:143
  280.2 72.5 %copy-start.74 = (f32[768]{0:T(1024)}, f32[768]{0:T(1024)S(1)}, u32[]{:S(2)}) copy-start(f32[768]{0:T(1024)S(1)} %convert_element_type.159) | copy-start | bytes 9220
  344.3 10.1 copy-start.86
  358.9 181.8 %all-gather.9.cloned.1.call-start = ((), (), s32[]{:S(2)}) async-start(), calls=%async_computation.8 | async-start | bytes 3932160 | tf_op jit(solution)/shard_map/all_gather | solution.py:154
  361.3 109.5 %copy-start.26 = (bf16[512,768]{1,0:T(8,128)(2,1)S(1)}, bf16[512,768]{1,0:T(8,128)(2,1)}, u32[]{:S(2)}) copy-start(bf16[512,768]{1,0:T(8,128)(2,1)} %param.29) | copy-start | bytes 2359300
  473.6 67.0 %copy-start.75 = (f32[768]{0:T(1024)S(1)}, f32[768]{0:T(1024)}, u32[]{:S(2)}) copy-start(f32[768]{0:T(1024)} %copy-done.74) | copy-start | bytes 9220
  476.4 189.7 %reduce-scatter.9.cloned.1.call-start = ((), (), s32[]{:S(2)}) async-start(), calls=%async_computation.9 | async-start | bytes 7864320 | tf_op jit(solution)/shard_map/reduce_scatter | solution.py:164
  556.6 109.6 %copy-start.49 = (f32[768]{0:T(1024)S(1)}, f32[768]{0:T(1024)}, u32[]{:S(2)}) copy-start(f32[768]{0:T(1024)} %convert_element_type.155) | copy-start | bytes 9220
  556.6 109.6 %copy-start.51 = (f32[512]{0:T(512)S(1)}, f32[512]{0:T(512)}, u32[]{:S(2)}) copy-start(f32[512]{0:T(512)} %copy-done.50) | copy-start | bytes 6148
  556.6 109.6 %copy-start.54 = (f32[512]{0:T(512)S(1)}, f32[512]{0:T(512)}, u32[]{:S(2)}) copy-start(f32[512]{0:T(512)} %copy-done.53) | copy-start | bytes 6148
  556.6 112.9 %copy-start.58 = (f32[512]{0:T(512)S(1)}, f32[512]{0:T(512)}, u32[]{:S(2)}) copy-start(f32[512]{0:T(512)} %copy-done.57) | copy-start | bytes 6148
  556.6 180.5 %all-gather.11.cloned.1.call-start = ((), (), s32[]{:S(2)}) async-start(), calls=%async_computation.10 | async-start | bytes 3932160 | tf_op jit(solution)/shard_map/all_gather | solution.py:171
  669.5 67.7 %copy-start.31 = (bf16[192,768]{1,0:T(8,128)(2,1)S(1)}, bf16[192,768]{1,0:T(8,128)(2,1)}, u32[]{:S(2)}) copy-start(bf16[192,768]{1,0:T(8,128)(2,1)} %param.19) | copy-start | bytes 884740
  670.2 70.1 %copy-start.59 = (f32[512]{0:T(512)}, f32[512]{0:T(512)S(1)}, u32[]{:S(2)}) copy-start(f32[512]{0:T(512)S(1)} %negate_multiply_fusion) | copy-start | bytes 6148
  673.0 248.5 %reduce-scatter.11.cloned.1.call-start = ((), (), s32[]{:S(2)}) async-start(), calls=%async_computation.11 | async-start | bytes 3932160 | tf_op jit(solution)/shard_map/reduce_scatter | solution.py:183
  742.9 12.0 %copy-start.7 = (f32[1,32,64,3,1,64]{5,2,3,1,4,0:T(8,128)S(1)}, f32[1,32,64,3,1,64]{5,2,3,1,4,0:T(8,128)}, u32[]{:S(2)}) copy-start(f32[1,32,64,3,1,64]{5,2,3,1,4,0:T(8,128)} %copy.191) | copy-start | bytes 4718596
  742.9 12.0 %copy-start.18 = (f32[1,32,64,3,64]{2,1,4,3,0:T(8,128)S(1)}, f32[1,32,64,3,64]{2,1,4,3,0:T(8,128)}, u32[]{:S(2)}) copy-start(f32[1,32,64,3,64]{2,1,4,3,0:T(8,128)} %reshape.798) | copy-start | bytes 4718596
  764.7 5.4 copy-start.33
  764.7 5.4 copy-start.38
  764.7 5.5 copy-start.3
  777.2 8.3 copy-start.63
  777.2 8.3 copy-start.66
  789.3 5.9 copy-start.5
  789.3 5.9 copy-start.28
  795.1 7.8 copy-start.13
  795.2 7.8 copy-start.22
  809.9 4.7 copy-start.20
  809.9 4.7 copy-start.25
  810.0 4.7 copy-start.52
  814.6 8.1 copy-start.9
  814.6 8.1 copy-start.10
  814.7 8.1 copy-start.45
  814.7 8.1 copy-start.47
  835.9 6.7 copy-start.87
  846.7 178.4 %all-reduce.8.cloned.1.call-start = ((), (), s32[]{:S(2)}) async-start(), calls=%async_computation.12 | async-start | bytes 14155776 | tf_op jit(solution)/shard_map/psum | solution.py:191
  847.0 7.1 copy-start.85
  847.0 7.1 copy-start.90
  854.1 4.2 copy-start.14
  863.7 43.8 %copy-start.76 = (f32[768]{0:T(1024)S(1)}, f32[768]{0:T(1024)}, u32[]{:S(2)}) copy-start(f32[768]{0:T(1024)} %get-tuple-element.40) | copy-start | bytes 9220
  863.7 57.8 %copy-start.16 = (f32[512,768]{1,0:T(8,128)S(1)}, f32[512,768]{1,0:T(8,128)}, u32[]{:S(2)}) copy-start(f32[512,768]{1,0:T(8,128)} %copy-done.15) | copy-start | bytes 4718596
  863.7 57.8 %copy-start.60 = (f32[512]{0:T(512)S(1)}, f32[512]{0:T(512)}, u32[]{:S(2)}) copy-start(f32[512]{0:T(512)} %copy-done.59) | copy-start | bytes 6148
  (36 other events, 73.9 us)
Sparse Core Ops, SparseCore 0:
  9.6 66.1 all-gather.4
  167.4 109.3 reduce-scatter.4
  280.3 64.0 all-gather.6
  359.0 109.3 reduce-scatter.6
  476.6 64.0 all-gather.8
  556.7 109.3 reduce-scatter.8
  673.1 64.0 all-gather.10
  846.8 59.8 reduce-scatter.10
  911.5 113.5 all-reduce.7
where the time goes:
time: 1050 us; the launch traced here: 1040 us
  waiting for transfers between devices  681 us (65%)
  matrix products  166 us (16%)
  local copies, waits for them, and re-layouts  73.7 us (7%)
  blocking collectives  57 us (5%)
  other arithmetic  45.5 us (4%)
  between operations  15.3 us (1%)
    reduce_scatter x1, waiting for transfers between devices, on_device(): lax.psum_scatter(rows_back(d_hidden, w_in), 'tensor', scatter_dimension=0...  109 us
    reduce_scatter x1, waiting for transfers between devices, on_device(): lax.psum_scatter(rows_product(attended, w_out), 'tensor', scatter_dimensi...  107 us
    reduce_scatter x1, waiting for transfers between devices, on_device(): lax.psum_scatter(rows_product(active, w_two), 'tensor', scatter_dimension...  107 us
    psum x1, waiting for transfers between devices, on_device(): lax.psum((d_w_qkv, d_b_qkv, d_w_out, d_w_in, d_b_in, d_w_two), 'dp')  101 us
    all_gather x1, waiting for transfers between devices, on_device(): second_full = lax.all_gather(d_second, 'tensor', axis=0, tiled=True)  64.1 us
    all_gather x1, waiting for transfers between devices, on_device(): middle_full = lax.all_gather(first_low, 'tensor', axis=0, tiled=True)  64.1 us
    all_gather x1, waiting for transfers between devices, on_device(): branch_full = lax.all_gather(d_branch, 'tensor', axis=0, tiled=True)  63.5 us
    all_gather x1, waiting for transfers between devices, on_device(): input_full = lax.all_gather(tokens, 'tensor', axis=0, tiled=True)  63.1 us
  transfers between devices with their start and end apart: 9, of which 8 were waited for; matrix products, arithmetic and copies ran while one was open for 3% of the time, Pallas kernels for 0%

commit v1 on v0

--- a/solution.py
+++ b/solution.py
@@ -146,12 +146,17 @@
     second_sum = first_low.astype(jnp.float32) + second
     block_out = normalize(second_sum, gain_b, shift_b).astype(jnp.bfloat16)
     input_back = lax.all_gather(tokens, "tensor", axis=0, tiled=True)
-    middle_back = lax.all_gather(first_low, "tensor", axis=0, tiled=True)
     unused_two, norm_two_back = jax.vjp(normalize, second_sum, gain_b, shift_b)
     d_r2, d_gain_two, d_shift_two = norm_two_back(cotangent.astype(jnp.float32))
     d_second = d_r2.astype(jnp.bfloat16)
     d_b_two = jnp.sum(d_second, axis=0, dtype=jnp.float32)
-    second_full = lax.all_gather(d_second, "tensor", axis=0, tiled=True)
+    middle_back, second_full = jnp.split(
+        jax.lax.all_gather(
+            jnp.concatenate([first_low, d_second], axis=1), "tensor", tiled=True, axis=0
+        ),
+        [first_low.shape[1]],
+        axis=1,
+    )
     hidden_again = jnp.dot(middle_back, w_in, preferred_element_type=jnp.float32) + bias_in
     active_val, gelu_back = jax.vjp(smooth, hidden_again)
     active_again = active_val.astype(jnp.bfloat16)

time: 1050 us -> 1090 us (1.038)
  waiting for transfers between devices: 681 us -> 728 us
    all_gather x1, waiting for transfers between devices: 64.1 us -> 116 us  [on_device(): jax.lax.all_gather(jnp.concatenate([first_low, d_second], axis=1), 'tenso...]
    unnamed x189 -> x191, local copies, waits for them, and re-layouts: 29.2 us -> 27.7 us
where the time goes in v1:
time: 1090 us
  waiting for transfers between devices  728 us (67%)
  matrix products  169 us (16%)
  local copies, waits for them, and re-layouts  72.2 us (7%)
  blocking collectives  57.1 us (5%)
  other arithmetic  45.9 us (4%)
  between operations  15.4 us (1%)
    all_gather x1, waiting for transfers between devices, on_device(): jax.lax.all_gather(jnp.concatenate([first_low, d_second], axis=1), 'tenso...  116 us
    reduce_scatter x1, waiting for transfers between devices, on_device(): lax.psum_scatter(rows_back(d_hidden, w_in), 'tensor', scatter_dimension=0...  109 us
    reduce_scatter x1, waiting for transfers between devices, on_device(): lax.psum_scatter(rows_product(active, w_two), 'tensor', scatter_dimension...  107 us
    reduce_scatter x1, waiting for transfers between devices, on_device(): lax.psum_scatter(rows_product(attended, w_out), 'tensor', scatter_dimensi...  107 us
    psum x1, waiting for transfers between devices, on_device(): lax.psum((d_w_qkv, d_b_qkv, d_w_out, d_w_in, d_b_in, d_w_two), 'dp')  96.9 us
    all_gather x1, waiting for transfers between devices, on_device(): middle_full = lax.all_gather(first_low, 'tensor', axis=0, tiled=True)  64.1 us
    all_gather x1, waiting for transfers between devices, on_device(): branch_full = lax.all_gather(d_branch, 'tensor', axis=0, tiled=True)  63.5 us
    all_gather x1, waiting for transfers between devices, on_device(): input_full = lax.all_gather(tokens, 'tensor', axis=0, tiled=True)  63.1 us
  transfers between devices with their start and end apart: 9, of which 8 were waited for; matrix products, arithmetic and copies ran while one was open for 3% of the time, Pallas kernels for 0%

profile of v1, /device:TPU:0, one launch (start us, length us, event | category | flops | bytes accessed | tf_op | source)
XLA Modules:
  0.0 1087.9 jit_solution(12424413140488585899)
XLA Ops:
  12.7 63.1 %all-gather.5.cloned.1.call-done = bf16[2048,768]{1,0:T(8,128)(2,1)} async-done(((bf16[512,768]{1,0:T(8,128)(2,1)}), bf16[2048,768]{1,0:T(8,128)(2,1)}) %all-gather.5.cloned.1.call-update) | async-done | bytes 3145744 | tf_op jit(solution)/shard_map/all_gather | solution.py:132
  75.8 6.3 convolution_add_fusion
  82.2 8.7 reshape_reshape.3
  90.9 8.1 fusion.127
  99.0 3.9 copy.193
  102.9 3.9 copy.191
  106.8 4.0 copy.192
  110.8 5.0 bitcast_multiply_fusion.4
  115.8 3.8 maximum_bitcast_fusion
  121.2 2.6 copy-done.6
  123.8 6.0 fusion.40
  129.8 4.1 fusion.36
  133.9 5.0 fusion.97
  138.9 5.4 multiply_reduce_fusion.1
  144.3 5.4 fusion.32
  150.5 9.2 divide_convert_fusion
  160.7 1.7 convert_element_type.155
  162.4 4.8 fusion.128
  169.7 107.1 %reduce-scatter.5.cloned.1.call-done = f32[512,768]{1,0:T(8,128)} async-done(((f32[2048,768]{1,0:T(8,128)}), f32[512,768]{1,0:T(8,128)}) %reduce-scatter.5.cloned.1.call-update) | async-done | bytes 1572880 | tf_op jit(solution)/shard_map/reduce_scatter | solution.py:135
  276.8 1.7 fusion.125
  280.2 64.1 %all-gather.7.cloned.1.call-done = bf16[2048,768]{1,0:T(8,128)(2,1)} async-done(((bf16[512,768]{1,0:T(8,128)(2,1)}), bf16[2048,768]{1,0:T(8,128)(2,1)}) %all-gather.7.cloned.1.call-update) | async-done | bytes 3145744 | tf_op jit(solution)/shard_map/all_gather | solution.py:140
  344.3 9.4 fusion.86
  356.3 107.1 %reduce-scatter.7.cloned.1.call-done = f32[512,768]{1,0:T(8,128)} async-done(((f32[2048,768]{1,0:T(8,128)}), f32[512,768]{1,0:T(8,128)}) %reduce-scatter.7.cloned.1.call-update) | async-done | bytes 1572880 | tf_op jit(solution)/shard_map/reduce_scatter | solution.py:143
  463.4 2.0 fusion.124
  467.0 1.6 fusion.123
  471.9 116.0 %all-gather.9.cloned.1.call-done = bf16[2048,1536]{1,0:T(8,128)(2,1)} async-done(((bf16[512,1536]{1,0:T(8,128)(2,1)}), bf16[2048,1536]{1,0:T(8,128)(2,1)}) %all-gather.9.cloned.1.call-update) | async-done | bytes 6291472 | tf_op jit(solution)/shard_map/all_gather | solution.py:154
  587.8 4.7 fusion.51
  592.6 7.1 convert_reduce_fusion.1
  599.7 1.8 copy-done.90
  601.4 4.5 fusion.129
  606.1 109.1 %reduce-scatter.9.cloned.1.call-done = f32[512,768]{1,0:T(8,128)} async-done(((f32[2048,768]{1,0:T(8,128)}), f32[512,768]{1,0:T(8,128)}) %reduce-scatter.9.cloned.1.call-update) | async-done | bytes 1572880 | tf_op jit(solution)/shard_map/reduce_scatter | solution.py:169
  715.1 3.3 multiply_reduce_fusion.2
  720.3 1.7 convert_reduce_fusion.4
  722.7 63.5 %all-gather.11.cloned.1.call-done = bf16[2048,768]{1,0:T(8,128)(2,1)} async-done(((bf16[512,768]{1,0:T(8,128)(2,1)}), bf16[2048,768]{1,0:T(8,128)(2,1)}) %all-gather.11.cloned.1.call-update) | async-done | bytes 3145744 | tf_op jit(solution)/shard_map/all_gather | solution.py:176
  786.2 3.1 fusion.130
  789.2 2.6 reshape.798
  791.9 12.0 %fusion.29 = f32[32,3,64,64]{2,3,1,0:T(8,128)} fusion(f32[32,3,64,64]{2,3,1,0:T(8,128)} %copy-done.21, f32[32,64,64]{1,2,0:T(8,128)S(1)} %copy-done.12, f32[1,32,64,3,64]{2,1,4,3,0:T(8,128)} %reshape.798, f32[32,64,3]{1,2,0:T(4,128)S(1)} %copy-done.43), kind=kOutput, calls=%fused_computation.47 | convolution fusion | flops 302776320 | bytes 5267456 | tf_op jit(solution)/shard_map/transpose(jvp(vmap(bhij,bjhd->bihd)))/dot_general | solution.py:48
  803.9 7.3 fusion.27
  811.2 2.4 reshape.793
  813.6 5.4 multiply_reduce_fusion
  819.1 2.7 fusion.95
  822.1 3.9 copy.158
  826.0 8.3 fusion.60
  834.4 3.7 fusion.63
  838.1 5.8 fusion.39
  844.0 7.7 fusion.21
  851.8 7.1 fusion.47
  858.9 4.6 bitcast_add_fusion
  863.7 8.1 add_bitcast_fusion
  871.8 2.8 fusion.20
  874.6 2.9 convert_reduce_fusion
  877.5 7.4 copy.171
  884.9 6.7 convert_element_type.172
  891.6 4.1 convolution_convert_fusion
  896.0 7.0 fusion.49
  903.1 8.7 fusion.38
  911.8 1.6 fusion.131
  914.0 3.2 convolution_bitcast_fusion
  918.0 42.7 %all-reduce.3 = (f32[768]{0:T(1024)}, f32[768]{0:T(1024)}, f32[768]{0:T(1024)}, f32[768]{0:T(1024)}, f32[768]{0:T(1024)}, /*index=5*/f32[768]{0:T(1024)}) all-reduce(f32[768]{0:T(1024)S(1)} %copy-done.72, f32[768]{0:T(1024)S(1)} %copy-done.73, f32[768]{0:T(1024)S(1)} %copy-done.74, ...), channel_id=1, replica_groups=mesh['dp'=8,'tensor'=4] {'dp','tensor'}, use_global_device_ids=true, to_apply=%region_22.23 | all-reduce | flops 4608 | bytes 36864 | tf_op jit(solution)/shard_map/psum | solution.py:199
  960.8 14.3 %all-reduce.4 = (f32[576]{0:T(1024)}, f32[768]{0:T(1024)}) all-reduce(f32[576]{0:T(1024)S(1)} %reduce_sum.223, f32[768]{0:T(1024)S(1)} %copy-done.78), channel_id=1, replica_groups=mesh['dp'=8,'tensor'=4] {'dp'}, use_global_device_ids=true, to_apply=%region_19.20 | all-reduce | flops 1344 | bytes 10752 | tf_op jit(solution)/shard_map/psum | solution.py:196
  975.1 2.3 add_convert_fusion.1
  977.4 96.9 %all-reduce.8.cloned.1.call-done = (f32[768,576]{0,1:T(8,128)}, f32[192,768]{1,0:T(8,128)}, f32[768,768]{1,0:T(8,128)}, f32[768,768]{1,0:T(8,128)}) async-done(((f32[768,576]{0,1:T(8,128)}, f32[192,768]{1,0:T(8,128)}, f32[768,768]{1,0:T(8,128)}, f32[768,768]{1,0:T(8,128)}), (f32[768,576]{0,1:T(8,128)}, f32[192,768]{1,0:T(8,128)}, f32[768,768]{1,0:T(8,128)}, ...) | async-done | bytes 7077904 | tf_op jit(solution)/shard_map/psum | solution.py:196
  1074.3 2.9 copy.250
  1078.1 1.4 copy.252
  (252 shorter events, 26.9 us)
Async XLA Ops:
  7.2 337.1 %copy-start = (bf16[768,768]{1,0:T(8,128)(2,1)S(1)}, bf16[768,768]{1,0:T(8,128)(2,1)}, u32[]{:S(2)}) copy-start(bf16[768,768]{1,0:T(8,128)(2,1)} %param.23) | copy-start | bytes 3538948
  7.2 68.6 %all-gather.5.cloned.1.call-start = ((), (), s32[]{:S(2)}) async-start(), calls=%async_computation.4 | async-start | bytes 3932160 | tf_op jit(solution)/shard_map/all_gather | solution.py:132
  7.9 268.9 %reduce-scatter.5.cloned.1.call-start = ((), (), s32[]{:S(2)}) async-start(), calls=%async_computation.5 | async-start | bytes 7864320 | tf_op jit(solution)/shard_map/reduce_scatter | solution.py:135
  12.1 117.7 %copy-start.62 = (s32[32]{0:T(128)}, s32[32]{0:T(128)S(1)}, u32[]{:S(2)}) copy-start(s32[32]{0:T(128)S(1)} %get-tuple-element.20) | copy-start | bytes 388
  12.1 117.7 %copy-start.65 = (s32[32]{0:T(128)}, s32[32]{0:T(128)S(1)}, u32[]{:S(2)}) copy-start(s32[32]{0:T(128)S(1)} %get-tuple-element.21) | copy-start | bytes 388
  12.2 109.0 %copy-start.40 = (f32[32,64]{1,0:T(8,128)}, f32[32,64]{1,0:T(8,128)S(1)}, u32[]{:S(2)}) copy-start(f32[32,64]{1,0:T(8,128)S(1)} %get-tuple-element.55) | copy-start | bytes 24580
  12.3 98.5 %copy-start.45 = (f32[32,64]{1,0:T(8,128)}, f32[32,64]{1,0:T(8,128)S(1)}, u32[]{:S(2)}) copy-start(f32[32,64]{1,0:T(8,128)S(1)} %get-tuple-element.69) | copy-start | bytes 24580
  12.3 98.5 %copy-start.47 = (f32[32,64]{1,0:T(8,128)}, f32[32,64]{1,0:T(8,128)S(1)}, u32[]{:S(2)}) copy-start(f32[32,64]{1,0:T(8,128)S(1)} %get-tuple-element.70) | copy-start | bytes 24580
  12.7 131.6 %copy-start.11 = (f32[32,64,64]{1,2,0:T(8,128)}, f32[32,64,64]{1,2,0:T(8,128)S(1)}, u32[]{:S(2)}) copy-start(f32[32,64,64]{1,2,0:T(8,128)S(1)} %and_convert_fusion) | copy-start | bytes 1572868
  119.6 19.4 %copy-start.4 = (f32[32,64,3,128]{3,1,2,0:T(8,128)}, f32[32,64,3,128]{3,1,2,0:T(8,128)S(1)}, u32[]{:S(2)}) copy-start(f32[32,64,3,128]{3,1,2,0:T(8,128)S(1)} %get-tuple-element.79) | copy-start | bytes 9437188
  119.6 30.9 %copy-start.2 = (f32[32,64,3,128]{3,1,2,0:T(8,128)}, f32[32,64,3,128]{3,1,2,0:T(8,128)S(1)}, u32[]{:S(2)}) copy-start(f32[32,64,3,128]{3,1,2,0:T(8,128)S(1)} %get-tuple-element.78) | copy-start | bytes 9437188
  121.2 12.8 %copy-start.36 = (f32[32,3,128]{2,0,1:T(8,128)}, f32[32,3,128]{2,0,1:T(8,128)S(1)}, u32[]{:S(2)}) copy-start(f32[32,3,128]{2,0,1:T(8,128)S(1)} %fusion.92) | copy-start | bytes 147460
  133.9 16.5 %copy-start.19 = (f32[32,3,128,64]{2,0,3,1:T(8,128)}, f32[32,3,128,64]{2,0,3,1:T(8,128)S(1)}, u32[]{:S(2)}) copy-start(f32[32,3,128,64]{2,0,3,1:T(8,128)S(1)} %fusion.36) | copy-start | bytes 9437188
  138.9 10.9 copy-start.38
  144.3 5.5 copy-start.21
  144.3 5.5 copy-start.33
  150.5 9.2 copy-start.42
  162.3 4.9 copy-start.23
  167.2 109.6 %copy-start.28 = (bf16[512,768]{1,0:T(8,128)(2,1)S(1)}, bf16[512,768]{1,0:T(8,128)(2,1)}, u32[]{:S(2)}) copy-start(bf16[512,768]{1,0:T(8,128)(2,1)} %param.15) | copy-start | bytes 2359300
  167.3 177.1 %all-gather.7.cloned.1.call-start = ((), (), s32[]{:S(2)}) async-start(), calls=%async_computation.6 | async-start | bytes 3932160 | tf_op jit(solution)/shard_map/all_gather | solution.py:140
  278.5 75.2 %copy-start.51 = (f32[512]{0:T(512)}, f32[512]{0:T(512)S(1)}, u32[]{:S(2)}) copy-start(f32[512]{0:T(512)S(1)} %broadcast_multiply_fusion.1) | copy-start | bytes 6148
  278.9 74.9 %copy-start.58 = (f32[512]{0:T(512)}, f32[512]{0:T(512)S(1)}, u32[]{:S(2)}) copy-start(f32[512]{0:T(512)S(1)} %multiply_reduce_fusion.5) | copy-start | bytes 6148
  278.9 74.9 %copy-start.54 = (f32[512]{0:T(512)}, f32[512]{0:T(512)S(1)}, u32[]{:S(2)}) copy-start(f32[512]{0:T(512)S(1)} %fusion.105) | copy-start | bytes 6148
  280.1 183.3 %reduce-scatter.7.cloned.1.call-start = ((), (), s32[]{:S(2)}) async-start(), calls=%async_computation.7 | async-start | bytes 7864320 | tf_op jit(solution)/shard_map/reduce_scatter | solution.py:143
  280.2 73.6 %copy-start.75 = (f32[768]{0:T(1024)}, f32[768]{0:T(1024)S(1)}, u32[]{:S(2)}) copy-start(f32[768]{0:T(1024)S(1)} %convert_element_type.161) | copy-start | bytes 9220
  353.8 234.0 %all-gather.9.cloned.1.call-start = ((), (), s32[]{:S(2)}) async-start(), calls=%async_computation.8 | async-start | bytes 7864320 | tf_op jit(solution)/shard_map/all_gather | solution.py:154
  356.3 109.5 %copy-start.27 = (bf16[512,768]{1,0:T(8,128)(2,1)S(1)}, bf16[512,768]{1,0:T(8,128)(2,1)}, u32[]{:S(2)}) copy-start(bf16[512,768]{1,0:T(8,128)(2,1)} %param.29) | copy-start | bytes 2359300
  471.8 120.8 %copy-start.76 = (f32[768]{0:T(1024)S(1)}, f32[768]{0:T(1024)}, u32[]{:S(2)}) copy-start(f32[768]{0:T(1024)} %copy-done.75) | copy-start | bytes 9220
  471.8 243.3 %reduce-scatter.9.cloned.1.call-start = ((), (), s32[]{:S(2)}) async-start(), calls=%async_computation.9 | async-start | bytes 7864320 | tf_op jit(solution)/shard_map/reduce_scatter | solution.py:169
  587.8 4.7 copy-start.86
  587.8 4.8 copy-start.88
  592.6 7.1 copy-start.91
  606.0 109.2 %copy-start.50 = (f32[768]{0:T(1024)S(1)}, f32[768]{0:T(1024)}, u32[]{:S(2)}) copy-start(f32[768]{0:T(1024)} %convert_element_type.157) | copy-start | bytes 9220
  606.0 109.2 %copy-start.52 = (f32[512]{0:T(512)S(1)}, f32[512]{0:T(512)}, u32[]{:S(2)}) copy-start(f32[512]{0:T(512)} %copy-done.51) | copy-start | bytes 6148
  606.0 109.2 %copy-start.55 = (f32[512]{0:T(512)S(1)}, f32[512]{0:T(512)}, u32[]{:S(2)}) copy-start(f32[512]{0:T(512)} %copy-done.54) | copy-start | bytes 6148
  606.0 112.4 %copy-start.59 = (f32[512]{0:T(512)S(1)}, f32[512]{0:T(512)}, u32[]{:S(2)}) copy-start(f32[512]{0:T(512)} %copy-done.58) | copy-start | bytes 6148
  606.0 180.1 %all-gather.11.cloned.1.call-start = ((), (), s32[]{:S(2)}) async-start(), calls=%async_computation.10 | async-start | bytes 3932160 | tf_op jit(solution)/shard_map/all_gather | solution.py:176
  718.5 67.7 %copy-start.32 = (bf16[192,768]{1,0:T(8,128)(2,1)S(1)}, bf16[192,768]{1,0:T(8,128)(2,1)}, u32[]{:S(2)}) copy-start(bf16[192,768]{1,0:T(8,128)(2,1)} %param.19) | copy-start | bytes 884740
  719.1 70.1 %copy-start.60 = (f32[512]{0:T(512)}, f32[512]{0:T(512)S(1)}, u32[]{:S(2)}) copy-start(f32[512]{0:T(512)S(1)} %negate_multiply_fusion) | copy-start | bytes 6148
  722.0 253.2 %reduce-scatter.11.cloned.1.call-start = ((), (), s32[]{:S(2)}) async-start(), calls=%async_computation.11 | async-start | bytes 3932160 | tf_op jit(solution)/shard_map/reduce_scatter | solution.py:188
  791.9 12.0 %copy-start.7 = (f32[1,32,64,3,1,64]{5,2,3,1,4,0:T(8,128)S(1)}, f32[1,32,64,3,1,64]{5,2,3,1,4,0:T(8,128)}, u32[]{:S(2)}) copy-start(f32[1,32,64,3,1,64]{5,2,3,1,4,0:T(8,128)} %copy.191) | copy-start | bytes 4718596
  791.9 12.0 %copy-start.18 = (f32[1,32,64,3,64]{2,1,4,3,0:T(8,128)S(1)}, f32[1,32,64,3,64]{2,1,4,3,0:T(8,128)}, u32[]{:S(2)}) copy-start(f32[1,32,64,3,64]{2,1,4,3,0:T(8,128)} %reshape.798) | copy-start | bytes 4718596
  813.6 5.4 copy-start.34
  813.6 5.4 copy-start.39
  813.6 5.5 copy-start.3
  826.0 8.3 copy-start.64
  826.0 8.3 copy-start.67
  838.1 5.9 copy-start.5
  838.1 5.9 copy-start.29
  844.0 7.8 copy-start.13
  844.0 7.8 copy-start.22
  858.9 4.7 copy-start.53
  863.6 8.1 copy-start.9
  863.6 8.1 copy-start.10
  863.6 8.1 copy-start.46
  863.6 8.1 copy-start.48
  884.9 6.7 copy-start.89
  895.7 7.4 copy-start.77
  895.7 178.6 %all-reduce.8.cloned.1.call-start = ((), (), s32[]{:S(2)}) async-start(), calls=%async_computation.12 | async-start | bytes 14155776 | tf_op jit(solution)/shard_map/psum | solution.py:196
  903.1 8.7 copy-start.14
  903.1 8.7 copy-start.24
  917.2 43.5 %copy-start.78 = (f32[768]{0:T(1024)S(1)}, f32[768]{0:T(1024)}, u32[]{:S(2)}) copy-start(f32[768]{0:T(1024)} %get-tuple-element.76) | copy-start | bytes 9220
  917.3 57.9 %copy-start.16 = (f32[512,768]{1,0:T(8,128)S(1)}, f32[512,768]{1,0:T(8,128)}, u32[]{:S(2)}) copy-start(f32[512,768]{1,0:T(8,128)} %copy-done.15) | copy-start | bytes 4718596
  917.3 57.9 %copy-start.61 = (f32[512]{0:T(512)S(1)}, f32[512]{0:T(512)}, u32[]{:S(2)}) copy-start(f32[512]{0:T(512)} %copy-done.60) | copy-start | bytes 6148
  (37 other events, 81.0 us)
Sparse Core Ops, SparseCore 0:
  9.6 66.1 all-gather.4
  167.4 109.3 reduce-scatter.4
  280.2 64.0 all-gather.6
  354.0 109.3 reduce-scatter.6
  471.9 115.8 all-gather.8
  606.1 108.9 reduce-scatter.8
  722.1 64.0 all-gather.10
  895.8 59.8 reduce-scatter.10
  960.5 113.7 all-reduce.7
